TPU v7x, 32 devices: a whole 2x2x4 slice. The times are simulated.
32 devices in a mesh: row: 8 (over y, x, core), col: 4 (over z).
Axes of the slice: x: 2, y: 2, z: 4, core: 2. Of those that a mesh axis runs over, the one named last changes fastest.
Arguments:
- loads: float32 [3, 24576], P(None, 'row'), may hold values from -6 to 6
- nd_source: int32 [24576], P('row'), may hold values from 0 to 24575, as said below
- panel: bfloat16 [24576, 512], P('row', 'col'), as said below
- trailing: bfloat16 [24576, 24576], P('row', 'col'), may hold values from -6 to 6
- pattern: int32 [192, 192], P('row', 'col'), may hold values from 0 to 1
- owner: int32 [8], replicated, may hold values from 0 to 7, each once
Outputs:
- loads_out: float32 [3, 24576], P(None, 'row')
- trailing_out: bfloat16 [24576, 24576], P('row', 'col')
Inputs may be any that keep to these rules, and one draw needn't show every extreme that they name: `nd_source`: a permutation; the rows t * 3072 to (t + 1) * 3072 - 1 take, from each block s of 3072 columns, exactly the columns s * 3072 + t * 384 to s * 3072 + (t + 1) * 384 - 1. `panel`: the 512 x 512 block at rows owner[0] * 3072 has a positive definite symmetric part. `owner`: a permutation of the row indices.
All inputs are finite; a program needn't handle non-finite values.
Results may differ from a plain program's by a relative error of at most 0.005.
Values may be sent and summed in bfloat16 or wider, within the bound.
A program may use at most 256 MiB of HBM per device.

v0:
```python
import jax
import jax.numpy as jnp
from jax import lax
from jax.sharding import PartitionSpec as P


def broadcast(array, axis, root):
    mine = lax.axis_index(axis) == root
    return lax.psum(jnp.where(mine, array, jnp.zeros_like(array)), axis)


def per_device(loads, nd_source, panel, trailing, pattern, owner):
    row_dev = panel.shape[0]
    row_count = lax.axis_size("row")
    col_count = lax.axis_size("col")
    pivot_size = panel.shape[1] * col_count
    share_size = row_dev // row_count
    row_place = lax.axis_index("row")
    col_place = lax.axis_index("col")
    arrived = lax.all_to_all(loads, "row", split_axis=1, concat_axis=1, tiled=True)
    source_slot = nd_source // row_dev * share_size + (nd_source % row_dev - row_place * share_size)
    regrouped = jnp.take(arrived, source_slot, axis=1)
    panel_rows = lax.all_gather(panel, "col", axis=1, tiled=True)
    owner_row = owner[0]
    pivot_block, pivot_loads = (
        broadcast(
            panel_rows[:pivot_size].astype(jnp.float32).astype(jnp.bfloat16), "row", owner_row
        ).astype(jnp.float32),
        broadcast(regrouped[:, :pivot_size].astype(jnp.bfloat16), "row", owner_row).astype(
            jnp.float32
        ),
    )
    symmetric = 0.5 * (pivot_block + pivot_block.T)
    lower_factor = jnp.linalg.cholesky(symmetric)
    inverse = lax.linalg.triangular_solve(
        lower_factor, jnp.eye(pivot_size, dtype=jnp.float32), left_side=True, lower=True
    )
    inverse_half = inverse.astype(jnp.bfloat16)
    factor_rows = jnp.dot(panel_rows, inverse_half.T, preferred_element_type=jnp.float32).astype(
        jnp.bfloat16
    )
    pivot_solve = jnp.dot(inverse, pivot_loads.T, precision=lax.Precision.HIGHEST)
    update = jnp.dot(
        factor_rows.astype(jnp.float32), pivot_solve, precision=lax.Precision.HIGHEST
    ).T
    pivot_start = owner_row * row_dev
    positions = row_place * row_dev + jnp.arange(row_dev, dtype=jnp.int32)
    in_pivot = (positions >= pivot_start) & (positions < pivot_start + pivot_size)
    pivot_offset = jnp.clip(positions - pivot_start, 0, pivot_size - 1)
    loads_out = jnp.where(
        in_pivot[None, :], jnp.take(pivot_solve.T, pivot_offset, axis=1), regrouped - update
    )
    holders = row_count // col_count
    pieces = []
    for member in range(holders):
        pieces.append(broadcast(factor_rows, "row", col_place * holders + member))
    factor_cols = jnp.concatenate(pieces, axis=0)
    block_rows = pattern.shape[0]
    block_cols = pattern.shape[1]
    block_size = trailing.shape[0] // block_rows
    col_dev = trailing.shape[1]
    product = jnp.einsum("ik,jk->ij", factor_rows, factor_cols, preferred_element_type=jnp.float32)
    masked = (
        product.reshape(block_rows, block_size, block_cols, block_size)
        * pattern.astype(jnp.float32)[:, None, :, None]
    ).reshape(row_dev, col_dev)
    trailing_out = (trailing.astype(jnp.float32) - masked).astype(jnp.bfloat16)
    return (loads_out, trailing_out)


def solution(mesh):
    return jax.shard_map(
        per_device,
        mesh=mesh,
        in_specs=(P(None, "row"), P("row"), P("row", "col"), P("row", "col"), P("row", "col"), P()),
        out_specs=(P(None, "row"), P("row", "col")),
        check_vma=False,
    )
```

profile of v0, /device:TPU:0, one launch (start us, length us, event | category | flops | bytes accessed | tf_op | source)
XLA Modules:
  0.0 477.6 jit_solution(12243766047315229716)
XLA Ops:
  7.2 2.3 copy.22
  10.2 66.1 %all-gather.2.cloned.1.call-done = bf16[3072,512]{0,1:T(8,128)(2,1)} async-done(((bf16[3072,128]{0,1:T(8,128)(2,1)}), bf16[3072,512]{0,1:T(8,128)(2,1)}) %all-gather.2.cloned.1.call-update) | async-done | bytes 3145744 | tf_op jit(solution)/shard_map/all_gather | solution.py:23
  76.3 1.9 slice_select_fusion
  78.3 0.8 iota_compare_fusion
  79.1 0.1 fusion.19
  79.2 54.3 %all-reduce.5.cloned.1.call-done = bf16[512,512]{0,1:T(8,128)(2,1)} async-done(((bf16[512,512]{0,1:T(8,128)(2,1)}), bf16[512,512]{0,1:T(8,128)(2,1)}) %all-reduce.5.cloned.1.call-update) | async-done | bytes 524304 | tf_op jit(solution)/shard_map/psum | solution.py:9
  133.4 1.3 copy.23
  134.7 1.2 fusion.7
  135.9 0.3 copy.24
  136.3 0.2 fusion.6
  136.5 1.0 copy-done
  137.5 11.7 %cholesky.104 = f32[128,128]{1,0:T(8,128)S(1)} custom-call(f32[128,128]{1,0:T(8,128)S(1)} %cholesky.266), custom_call_target="Cholesky" | custom-call | tf_op jit(solution)/shard_map/jit(cholesky)/cholesky | solution.py:34
  149.2 9.8 %custom-call.30 = f32[1,128,128]{1,2,0:T(8,128)S(1)} custom-call(f32[1,128,128]{2,1,0:T(8,128)S(1)} %get-tuple-element.35), custom_call_target="InvertDiagBlocksLowerTriangular" | custom-call | tf_op jit(solution)/shard_map/jit(cholesky)/cholesky | solution.py:34
  159.0 0.1 cholesky.224
  159.2 1.2 constant_dynamic-update-slice_fusion.2
  160.4 1.3 convolution_subtract_fusion.4
  161.7 11.7 %cholesky.217 = f32[128,128]{1,0:T(8,128)S(1)} custom-call(f32[128,128]{1,0:T(8,128)S(1)} %cholesky.270), custom_call_target="Cholesky" | custom-call | tf_op jit(solution)/shard_map/jit(cholesky)/cholesky | solution.py:34
  173.4 10.2 %custom-call.31 = f32[1,128,128]{1,2,0:T(8,128)S(1)} custom-call(f32[1,128,128]{2,1,0:T(8,128)S(1)} %get-tuple-element.32), custom_call_target="InvertDiagBlocksLowerTriangular" | custom-call | tf_op jit(solution)/shard_map/jit(cholesky)/cholesky | solution.py:34
  183.7 0.3 convolution_dynamic-update-slice_fusion
  183.9 1.3 convolution_subtract_fusion.5
  185.2 11.7 %cholesky.238 = f32[128,128]{1,0:T(8,128)S(1)} custom-call(f32[128,128]{1,0:T(8,128)S(1)} %cholesky.275), custom_call_target="Cholesky" | custom-call | tf_op jit(solution)/shard_map/jit(cholesky)/cholesky | solution.py:34
  197.0 0.6 compare_reduce_fusion.1
  197.6 9.8 %custom-call.32 = f32[1,128,128]{1,2,0:T(8,128)S(1)} custom-call(f32[1,128,128]{2,1,0:T(8,128)S(1)} %get-tuple-element.29), custom_call_target="InvertDiagBlocksLowerTriangular" | custom-call | tf_op jit(solution)/shard_map/jit(cholesky)/cholesky | solution.py:34
  207.4 0.2 convolution_dynamic-update-slice_fusion.1
  207.6 1.2 convolution_subtract_fusion.6
  208.9 11.8 %cholesky.255 = f32[128,128]{1,0:T(8,128)S(1)} custom-call(f32[128,128]{1,0:T(8,128)S(1)} %convolution_subtract_fusion.6), custom_call_target="Cholesky" | custom-call | tf_op jit(solution)/shard_map/jit(cholesky)/cholesky | solution.py:34
  220.7 0.7 compare_reduce_fusion
  221.4 0.7 compare_reduce_fusion.2
  224.6 0.1 select_select_fusion
  224.8 7.6 %while.1 = (s32[]{:T(128)}, f32[512,512]{1,0:T(8,128)S(1)}, s32[4,2]{0,1:T(2,128)S(1)}, f32[4,128,128]{2,1,0:T(8,128)S(1)}, s32[]{:T(128)}) while((s32[]{:T(128)}, f32[512,512]{1,0:T(8,128)S(1)}, s32[4,2]{0,1:T(2,128)S(1)}, f32[4,128,128]{2,1,0:T(8,128)S(1)}, s32[]{:T(128)}) %tuple.34), condition=%wide.while_cond, body=%wide.while_body.sunk | while | flops 2 | bytes 131189 | solution.py:35
  224.8 0.1 constant_dynamic-slice_fusion.2
  224.9 0.5 fusion.70
  225.4 1.3 bitcast_dynamic-update-slice_fusion.2
  226.8 0.5 fusion.70
  227.3 1.3 bitcast_dynamic-update-slice_fusion.2
  228.7 0.5 fusion.70
  229.2 1.3 bitcast_dynamic-update-slice_fusion.2
  230.6 0.5 fusion.70
  231.1 1.3 bitcast_dynamic-update-slice_fusion.2
  232.4 39.3 %custom-call.33 = f32[4,128,128]{1,2,0:T(8,128)S(1)} custom-call(f32[4,128,128]{2,1,0:T(8,128)S(1)} %get-tuple-element.9), custom_call_target="InvertDiagBlocksLowerTriangular" | custom-call | tf_op jit(solution)/shard_map/triangular_solve | solution.py:35
  271.7 1.2 fusion.21
  273.0 0.4 convolution_subtract_fusion.2
  273.3 0.4 fusion.33
  273.8 0.4 convolution_subtract_fusion.1
  274.2 0.4 fusion.31
  274.6 0.6 convolution_subtract_fusion.3
  275.3 0.4 fusion.30
  275.7 0.7 copy-done.3
  276.4 1.8 convolution_convert_fusion
  278.2 3.1 select_bitcast_fusion.1
  281.4 3.5 all-to-all-start
  285.1 5.1 %all-to-all-done = f32[3,8,384]{2,0,1:T(4,128)S(1)} async-done(((f32[3,8,384]{2,0,1:T(4,128)}), f32[3,8,384]{2,0,1:T(4,128)S(1)}, u32[]{:S(2)}, u32[]{:S(2)}) %all-to-all-start) | async-done | bytes 36896 | tf_op jit(solution)/shard_map/all_to_all | solution.py:20
  290.2 1.6 copy.25
  291.8 12.3 %gather_fusion = f32[3072,3]{1,0:T(8,128)} fusion(f32[3,3072]{0,1:T(8,128)} %bitcast.81, s32[3072]{0:T(1024)S(1)} %broadcast_clamp_fusion.1), kind=kCustom, calls=%fused_computation | custom fusion | bytes 86016 | tf_op jit(solution)/shard_map/jit(_take)/gather | solution.py:22
  304.1 1.9 copy.26
  306.1 12.3 %psum.29 = bf16[3,512]{1,0:T(4,128)(2,1)S(1)} all-reduce(bf16[3,512]{1,0:T(4,128)(2,1)S(1)} %fusion.49), channel_id=1, replica_groups=mesh['row'=8,'col'=4] {'row'}, use_global_device_ids=true, to_apply=%region_9.10 | all-reduce | flops 1536 | bytes 6144 | tf_op jit(solution)/shard_map/psum | solution.py:9
  318.4 1.7 fusion.14
  320.1 0.2 copy.27
  320.3 10.8 %gather_fusion.1 = f32[3072,3]{1,0:T(8,128)} fusion(f32[3,512]{0,1:T(8,128)S(1)} %copy.27, s32[3072]{0:T(1024)S(1)} %broadcast_clamp_fusion), kind=kCustom, calls=%fused_computation.1 | custom fusion | bytes 86016 | tf_op jit(solution)/shard_map/jit(_take)/gather | solution.py:51
  331.1 1.9 copy.28
  333.0 2.0 fusion.5
  334.9 50.3 %all-reduce.7.cloned.1.call-done = (bf16[3072,512]{0,1:T(8,128)(2,1)}, bf16[3072,512]{0,1:T(8,128)(2,1)}) async-done(((bf16[3072,512]{0,1:T(8,128)(2,1)}, bf16[3072,512]{0,1:T(8,128)(2,1)}), (bf16[3072,512]{0,1:T(8,128)(2,1)}, bf16[3072,512]{0,1:T(8,128)(2,1)})) %all-reduce.7.cloned.1.call-update) | async-done | bytes 6291472 | tf_op jit(solution)/shard_map/psum | solution.py:9
  385.2 23.8 %mul.44 = f32[24,128,48,128]{3,2,1,0:T(8,128)} broadcast(f32[24,48]{1,0:T(8,128)S(1)} %convert_element_type.36), dimensions={0,2} | broadcast | bytes 75502080 | tf_op jit(solution)/shard_map/mul | solution.py:64
  409.1 61.8 %fusion.1 = bf16[3072,6144]{1,0:T(8,128)(2,1)} fusion(f32[384,8,48,128]{3,2,1,0:T(8,128)} %bitcast.25, bf16[3072,6144]{1,0:T(8,128)(2,1)} %param.9, bf16[512,3072]{1,0:T(8,128)(2,1)S(1)} %convolution_convert_fusion, bf16[3072,512]{0,1:T(8,128)(2,1)} %get-tuple-element.18, bf16[3072,512]{0,1:T(8,128)(2,1)} %get-tuple-element.19), kind=kOutput, calls=%fused_computation.6 | convolution fusion | flops 19415433216 | bytes 160432128 | tf_op jit(solution)/shard_map/ik,jk->ij/dot_general | solution.py:62
  (41 shorter events, 0.7 us)
Async XLA Ops:
  7.2 69.2 %all-gather.2.cloned.1.call-start = ((), (), s32[]{:S(2)}) async-start(), calls=%async_computation.1 | async-start | bytes 3932160 | tf_op jit(solution)/shard_map/all_gather | solution.py:23
  9.5 123.9 %all-reduce.5.cloned.1.call-start = ((), (), s32[]{:S(2)}) async-start(), calls=%async_computation.2 | async-start | bytes 1048576 | tf_op jit(solution)/shard_map/psum | solution.py:9
  78.2 307.0 %all-reduce.7.cloned.1.call-start = ((), (), s32[]{:S(2)}) async-start(), calls=%async_computation.3 | async-start | bytes 12582912 | tf_op jit(solution)/shard_map/psum | solution.py:9
  136.5 1.0 copy-start
  271.7 4.7 copy-start.4
  273.8 1.9 copy-start.1
  274.6 1.1 copy-start.2
  275.7 0.7 copy-start.3
  281.4 3.5 copy-start.7
  281.4 3.6 copy-start.5
  281.4 3.7 copy-start.6
  281.4 8.8 %all-to-all-start = ((f32[3,8,384]{2,0,1:T(4,128)}), f32[3,8,384]{2,0,1:T(4,128)S(1)}, u32[]{:S(2)}, u32[]{:S(2)}) async-start(f32[3,8,384]{2,0,1:T(4,128)} %bitcast.13), calls=%async_computation | async-start | bytes 98304 | tf_op jit(solution)/shard_map/all_to_all | solution.py:20
Sparse Core Ops, SparseCore 0:
  10.1 66.1 all-gather.1
  80.0 53.4 all-reduce.4
  281.5 103.6 all-reduce.6
where the time goes:
time: 487 us; the launch traced here: 478 us
  waiting for transfers between devices  176 us (36%)
  other arithmetic  126 us (26%)
  matrix products  76.6 us (16%)
  local copies, waits for them, and re-layouts  65.7 us (13%)
  between operations  17.6 us (4%)
  blocking collectives  12.3 us (3%)
    psum x2, waiting for transfers between devices, broadcast(): return lax.psum(jnp.where(mine, array, jnp.zeros_like(array)), axis)  105 us
    another operation x14, other arithmetic, per_device(): lower_factor = jnp.linalg.cholesky(symmetric)  79 us
    all_gather x1, waiting for transfers between devices, per_device(): panel_rows = lax.all_gather(panel, 'col', axis=1, tiled=True)  66.1 us
    dot_general x1, matrix products, per_device(): jnp.einsum('ik,jk->ij', factor_rows, factor_cols, preferred_element_type=...  61.8 us
    another operation x3, other arithmetic, per_device(): lax.linalg.triangular_solve(lower_factor, jnp.eye(pivot_size, dtype=jnp.f...  39.4 us
    mul x1, local copies, waits for them, and re-layouts, per_device(): product.reshape(block_rows, block_size, block_cols, block_size)  23.8 us
    gather x2, local copies, waits for them, and re-layouts, per_device(): regrouped = jnp.take(arrived, source_slot, axis=1)  14.2 us
    gather x2, local copies, waits for them, and re-layouts, per_device(): jnp.take(pivot_solve.T, pivot_offset, axis=1)  12.7 us
  transfers between devices with their start and end apart: 4, of which 4 were waited for; matrix products, arithmetic and copies ran while one was open for 7% of the time, Pallas kernels for 0%

commit v1 on v0

--- a/solution.py
+++ b/solution.py
@@ -6,7 +6,7 @@
 
 def broadcast(array, axis, root):
     mine = lax.axis_index(axis) == root
-    return lax.psum(jnp.where(mine, array, jnp.zeros_like(array)), axis)
+    return jnp.sum(lax.all_gather(jnp.where(mine, array, jnp.zeros_like(array)), axis), axis=0)
 
 
 def per_device(loads, nd_source, panel, trailing, pattern, owner):

time: 487 us -> 670 us (1.38)
  waiting for transfers between devices: 176 us -> 263 us
  local copies, waits for them, and re-layouts: 65.7 us -> 121 us
  other arithmetic: 126 us -> 166 us
    all_gather x0 -> x3, waiting for transfers between devices: none -> 191 us  [broadcast(): lax.all_gather(jnp.where(mine, array, jnp.zeros_like(array)), axis)]
    psum x2 -> x0, waiting for transfers between devices: 105 us -> none  [broadcast(): return lax.psum(jnp.where(mine, array, jnp.zeros_like(array)), axis)]
    unnamed x17 -> x18, local copies, waits for them, and re-layouts: 3.98 us -> 56.1 us
    reduce_sum x0 -> x4, other arithmetic: none -> 41.3 us  [broadcast(): jnp.sum(lax.all_gather(jnp.where(mine, array, jnp.zeros_like(array)), axi...]
    psum x1 -> x0, blocking collectives: 12.3 us -> none  [broadcast(): return lax.psum(jnp.where(mine, array, jnp.zeros_like(array)), axis)]
    all_gather x0 -> x1, blocking collectives: none -> 9.04 us  [broadcast(): lax.all_gather(jnp.where(mine, array, jnp.zeros_like(array)), axis)]
  transfers between devices with their start and end apart: 4 -> 5, of which waited for: 4 -> 5; matrix products, arithmetic and copies ran while one was open for 7% -> 12% of each run, Pallas kernels for 0% -> 0%
where the time goes in v1:
time: 670 us; the launch traced here: 660 us
  waiting for transfers between devices  263 us (39%)
  other arithmetic  166 us (25%)
  local copies, waits for them, and re-layouts  121 us (18%)
  matrix products  79 us (12%)
  between operations  17.6 us (3%)
  blocking collectives  9.04 us (1%)
    all_gather x3, waiting for transfers between devices, broadcast(): lax.all_gather(jnp.where(mine, array, jnp.zeros_like(array)), axis)  191 us
    another operation x14, other arithmetic, per_device(): lower_factor = jnp.linalg.cholesky(symmetric)  78.8 us
    all_gather x1, waiting for transfers between devices, per_device(): panel_rows = lax.all_gather(panel, 'col', axis=1, tiled=True)  67.1 us
    dot_general x1, matrix products, per_device(): jnp.einsum('ik,jk->ij', factor_rows, factor_cols, preferred_element_type=...  62 us
    unnamed x18, local copies, waits for them, and re-layouts  56.1 us
    reduce_sum x4, other arithmetic, broadcast(): jnp.sum(lax.all_gather(jnp.where(mine, array, jnp.zeros_like(array)), axi...  41.3 us
    another operation x3, other arithmetic, per_device(): lax.linalg.triangular_solve(lower_factor, jnp.eye(pivot_size, dtype=jnp.f...  40.4 us
    mul x1, local copies, waits for them, and re-layouts, per_device(): product.reshape(block_rows, block_size, block_cols, block_size)  23.8 us
  transfers between devices with their start and end apart: 5, of which 5 were waited for; matrix products, arithmetic and copies ran while one was open for 12% of the time, Pallas kernels for 0%

profile of v1, /device:TPU:0, one launch (start us, length us, event | category | flops | bytes accessed | tf_op | source)
XLA Modules:
  0.0 659.6 jit_solution(14282092712034976379)
XLA Ops:
  7.2 0.7 all-gather.10.cloned.1.call-update
  8.6 67.1 %all-gather.10.cloned.1.call-done = bf16[3072,512]{1,0:T(8,128)(2,1)} async-done(((bf16[3072,128]{1,0:T(8,128)(2,1)}), bf16[3072,512]{1,0:T(8,128)(2,1)}) %all-gather.10.cloned.1.call-update) | async-done | bytes 3145744 | tf_op jit(solution)/shard_map/all_gather | solution.py:23
  75.7 1.9 slice_select_fusion
  77.9 35.1 %all-gather.12.cloned.1.call-done = bf16[4096,512]{1,0:T(8,128)(2,1)} async-done(((bf16[512,512]{1,0:T(8,128)(2,1)}), bf16[4096,512]{1,0:T(8,128)(2,1)}) %all-gather.12.cloned.1.call-update) | async-done | bytes 4194320 | tf_op jit(solution)/shard_map/all_gather | solution.py:9
  112.9 3.1 reduce_sum.48
  116.0 0.2 copy.18
  116.2 0.2 copy.19
  116.7 1.0 copy-done
  117.6 11.7 %cholesky.104 = f32[128,128]{1,0:T(8,128)S(1)} custom-call(f32[128,128]{1,0:T(8,128)S(1)} %cholesky.266), custom_call_target="Cholesky" | custom-call | tf_op jit(solution)/shard_map/jit(cholesky)/cholesky | solution.py:34
  129.4 9.8 %custom-call.30 = f32[1,128,128]{1,2,0:T(8,128)S(1)} custom-call(f32[1,128,128]{2,1,0:T(8,128)S(1)} %get-tuple-element.33), custom_call_target="InvertDiagBlocksLowerTriangular" | custom-call | tf_op jit(solution)/shard_map/jit(cholesky)/cholesky | solution.py:34
  139.3 1.2 constant_dynamic-update-slice_fusion.2
  140.6 1.3 convolution_subtract_fusion.4
  141.8 11.7 %cholesky.217 = f32[128,128]{1,0:T(8,128)S(1)} custom-call(f32[128,128]{1,0:T(8,128)S(1)} %cholesky.270), custom_call_target="Cholesky" | custom-call | tf_op jit(solution)/shard_map/jit(cholesky)/cholesky | solution.py:34
  153.6 10.0 %custom-call.31 = f32[1,128,128]{1,2,0:T(8,128)S(1)} custom-call(f32[1,128,128]{2,1,0:T(8,128)S(1)} %get-tuple-element.30), custom_call_target="InvertDiagBlocksLowerTriangular" | custom-call | tf_op jit(solution)/shard_map/jit(cholesky)/cholesky | solution.py:34
  163.6 0.3 convolution_dynamic-update-slice_fusion
  163.8 1.3 convolution_subtract_fusion.5
  165.1 11.7 %cholesky.238 = f32[128,128]{1,0:T(8,128)S(1)} custom-call(f32[128,128]{1,0:T(8,128)S(1)} %cholesky.275), custom_call_target="Cholesky" | custom-call | tf_op jit(solution)/shard_map/jit(cholesky)/cholesky | solution.py:34
  176.9 0.7 compare_reduce_fusion.1
  177.6 9.8 %custom-call.32 = f32[1,128,128]{1,2,0:T(8,128)S(1)} custom-call(f32[1,128,128]{2,1,0:T(8,128)S(1)} %get-tuple-element.27), custom_call_target="InvertDiagBlocksLowerTriangular" | custom-call | tf_op jit(solution)/shard_map/jit(cholesky)/cholesky | solution.py:34
  187.4 0.2 convolution_dynamic-update-slice_fusion.1
  187.6 1.2 convolution_subtract_fusion.6
  188.9 11.9 %cholesky.255 = f32[128,128]{1,0:T(8,128)S(1)} custom-call(f32[128,128]{1,0:T(8,128)S(1)} %convolution_subtract_fusion.6), custom_call_target="Cholesky" | custom-call | tf_op jit(solution)/shard_map/jit(cholesky)/cholesky | solution.py:34
  200.8 0.6 compare_reduce_fusion
  201.4 0.7 compare_reduce_fusion.2
  204.6 1.1 select_select_fusion
  205.7 11.7 %while.1 = (s32[]{:T(128)}, f32[512,512]{1,0:T(8,128)}, s32[4,2]{0,1:T(2,128)S(1)}, f32[4,128,128]{2,1,0:T(8,128)S(1)}, s32[]{:T(128)}) while((s32[]{:T(128)}, f32[512,512]{1,0:T(8,128)}, s32[4,2]{0,1:T(2,128)S(1)}, f32[4,128,128]{2,1,0:T(8,128)S(1)}, s32[]{:T(128)}) %tuple.34), condition=%wide.while_cond, body=%wide.while_body.sunk | while | flops 2 | bytes 131189 | solution.py:35
  205.8 0.6 fusion.71
  206.4 2.2 bitcast_dynamic-update-slice_fusion.2
  208.7 0.6 fusion.71
  209.3 2.2 bitcast_dynamic-update-slice_fusion.2
  211.7 0.6 fusion.71
  212.3 2.2 bitcast_dynamic-update-slice_fusion.2
  214.6 0.6 fusion.71
  215.2 2.2 bitcast_dynamic-update-slice_fusion.2
  217.4 39.3 %custom-call.33 = f32[4,128,128]{1,2,0:T(8,128)S(1)} custom-call(f32[4,128,128]{2,1,0:T(8,128)S(1)} %get-tuple-element.9), custom_call_target="InvertDiagBlocksLowerTriangular" | custom-call | tf_op jit(solution)/shard_map/triangular_solve | solution.py:35
  256.8 0.3 fusion.21
  257.1 1.4 convolution_subtract_fusion.2
  258.5 0.4 fusion.33
  258.9 1.4 convolution_subtract_fusion.1
  260.3 0.4 fusion.31
  260.8 1.7 convolution_subtract_fusion.3
  262.4 0.4 fusion.30
  262.9 0.7 copy-done.3
  263.6 1.8 convolution_convert_fusion
  265.4 3.1 select_bitcast_fusion.1
  268.6 0.5 all-gather.16.cloned.1.call-update
  269.1 3.4 all-to-all-start
  272.7 4.7 all-to-all-done
  277.3 1.7 copy.20
  279.1 12.4 %gather_fusion = f32[3072,3]{1,0:T(8,128)} fusion(f32[3,3072]{0,1:T(8,128)} %bitcast.95, s32[3072]{0:T(1024)S(1)} %broadcast_clamp_fusion.1), kind=kCustom, calls=%fused_computation | custom fusion | bytes 86016 | tf_op jit(solution)/shard_map/jit(_take)/gather | solution.py:22
  291.4 1.9 copy.21
  293.4 9.0 %all-gather.4 = bf16[8,3,512]{2,1,0:T(4,128)(2,1)S(1)} all-gather(bf16[1,3,512]{2,1,0:T(4,128)(2,1)S(1)} %fusion.50), channel_id=3, replica_groups=mesh['row'=8,'col'=4] {'row'}, dimensions={0}, use_global_device_ids=true | all-gather | bytes 27648 | tf_op jit(solution)/shard_map/all_gather | solution.py:9
  302.4 1.7 fusion.14
  304.3 10.8 %gather_fusion.1 = f32[3072,3]{1,0:T(8,128)} fusion(f32[3,512]{0,1:T(8,128)S(1)} %copy.22, s32[3072]{0:T(1024)S(1)} %broadcast_clamp_fusion), kind=kCustom, calls=%fused_computation.1 | custom fusion | bytes 86016 | tf_op jit(solution)/shard_map/jit(_take)/gather | solution.py:51
  315.1 1.9 copy.23
  317.0 2.0 fusion.5
  318.9 75.0 %all-gather.14.cloned.1.call-done = bf16[24576,512]{0,1:T(8,128)(2,1)} async-done(((bf16[3072,512]{0,1:T(8,128)(2,1)}), bf16[24576,512]{0,1:T(8,128)(2,1)}) %all-gather.14.cloned.1.call-update) | async-done | bytes 25165840 | tf_op jit(solution)/shard_map/all_gather | solution.py:9
  394.0 27.5 %copy.24 = bf16[64,8,8,3072]{3,2,1,0:T(8,128)(2,1)} copy(bf16[64,8,8,3072]{3,1,2,0:T(8,128)(2,1)} %bitcast.92) | data formatting | bytes 50331648
  421.5 19.1 %bitcast_reduce_fusion.1 = bf16[3072,512]{0,1:T(8,128)(2,1)} fusion(bf16[64,8,8,3072]{3,2,1,0:T(8,128)(2,1)} %copy.24), kind=kLoop, calls=%fused_computation.8 | loop fusion | flops 11010048 | bytes 28311552 | tf_op jit(solution)/shard_map/reduce_sum | solution.py:9
  440.6 80.4 %all-gather.16.cloned.1.call-done = bf16[24576,512]{0,1:T(8,128)(2,1)} async-done(((bf16[3072,512]{0,1:T(8,128)(2,1)}), bf16[24576,512]{0,1:T(8,128)(2,1)}) %all-gather.16.cloned.1.call-update) | async-done | bytes 25165840 | tf_op jit(solution)/shard_map/all_gather | solution.py:9
  521.0 26.9 %copy.25 = bf16[64,8,8,3072]{3,2,1,0:T(8,128)(2,1)} copy(bf16[64,8,8,3072]{3,1,2,0:T(8,128)(2,1)} %bitcast.93) | data formatting | bytes 50331648
  547.8 19.2 %bitcast_reduce_fusion = bf16[3072,512]{0,1:T(8,128)(2,1)} fusion(bf16[64,8,8,3072]{3,2,1,0:T(8,128)(2,1)} %copy.25), kind=kLoop, calls=%fused_computation.7 | loop fusion | flops 11010048 | bytes 28311552 | tf_op jit(solution)/shard_map/reduce_sum | solution.py:9
  567.0 23.8 %mul.42 = f32[24,128,48,128]{3,2,1,0:T(8,128)} broadcast(f32[24,48]{1,0:T(8,128)S(1)} %convert_element_type.54), dimensions={0,2} | broadcast | bytes 75502080 | tf_op jit(solution)/shard_map/mul | solution.py:64
  590.9 62.0 %fusion.1 = bf16[3072,6144]{1,0:T(8,128)(2,1)} fusion(f32[384,8,48,128]{3,2,1,0:T(8,128)} %bitcast.34, bf16[3072,6144]{1,0:T(8,128)(2,1)} %param.9, bf16[512,3072]{1,0:T(8,128)(2,1)S(1)} %convolution_convert_fusion, bf16[3072,512]{0,1:T(8,128)(2,1)} %bitcast_reduce_fusion, bf16[3072,512]{0,1:T(8,128)(2,1)} %bitcast_reduce_fusion.1), kind=kOutput, calls=%fused_computation.6 | convolution fusion | flops 19415433216 | bytes 160432128 | tf_op jit(solution)/shard_map/ik,jk->ij/dot_general | solution.py:62
  (48 shorter events, 1.5 us)
Async XLA Ops:
  7.2 68.5 %all-gather.10.cloned.1.call-start = ((), (), s32[]{:S(2)}) async-start(), calls=%async_computation.1 | async-start | bytes 3932160 | tf_op jit(solution)/shard_map/all_gather | solution.py:23
  7.9 105.1 %all-gather.12.cloned.1.call-start = ((), (), s32[]{:S(2)}) async-start(), calls=%async_computation.2 | async-start | bytes 4718592 | tf_op jit(solution)/shard_map/all_gather | solution.py:9
  77.6 316.4 %all-gather.14.cloned.1.call-start = ((), (), s32[]{:S(2)}) async-start(), calls=%async_computation.3 | async-start | bytes 28311552 | tf_op jit(solution)/shard_map/all_gather | solution.py:9
  116.6 1.0 copy-start
  256.8 6.8 %copy-start.4 = (bf16[3072,512]{1,0:T(8,128)(2,1)S(1)}, bf16[3072,512]{1,0:T(8,128)(2,1)}, u32[]{:S(2)}) copy-start(bf16[3072,512]{1,0:T(8,128)(2,1)} %all-gather.10.cloned.1.call-done) | copy-start | bytes 9437188
  258.9 4.0 copy-start.1
  260.8 2.1 copy-start.2
  262.9 0.7 copy-start.3
  268.5 4.0 copy-start.7
  268.5 4.1 copy-start.5
  268.5 4.2 copy-start.6
  268.5 252.4 %all-gather.16.cloned.1.call-start = ((), (), s32[]{:S(2)}) async-start(), calls=%async_computation.4 | async-start | bytes 28311552 | tf_op jit(solution)/shard_map/all_gather | solution.py:9
  269.1 8.2 %all-to-all-start = ((f32[3,8,384]{2,0,1:T(4,128)}), f32[3,8,384]{2,0,1:T(4,128)S(1)}, u32[]{:S(2)}, u32[]{:S(2)}) async-start(f32[3,8,384]{2,0,1:T(4,128)} %bitcast.13), calls=%async_computation | async-start | bytes 98304 | tf_op jit(solution)/shard_map/all_to_all | solution.py:20
Sparse Core Ops, SparseCore 0:
  9.5 66.1 all-gather.9
  78.1 34.7 all-gather.11
  268.7 125.2 all-gather.13
  395.7 125.1 all-gather.15
